TPU v7x, 128 devices: a whole 4x4x4 slice. The times are simulated.
128 devices in a mesh: gx: 8 (over z, core), gy: 16 (over x, y).
Axes of the slice: x: 4, y: 4, z: 4, core: 2. Of those that a mesh axis runs over, the one named last changes fastest.
Arguments:
- tokens: bfloat16 [4096, 4096], P(('gx', 'gy')), may hold values from -3 to 3
- attn_gain: bfloat16 [4096], replicated, may hold values from 0.099609375 to 1.8984375
- mlp_gain: bfloat16 [4096], replicated, may hold values from 0.099609375 to 1.8984375
- w_query: bfloat16 [4096, 4096], P('gx', 'gy'), may hold values from -1 to 1
- w_key: bfloat16 [4096, 1024], P('gx', 'gy'), may hold values from -1 to 1
- value_projection: bfloat16 [4096, 1024], P('gx', 'gy'), may hold values from -0.09375 to 0.09375
- w_out: bfloat16 [4096, 4096], P('gy', 'gx'), may hold values from -0.09375 to 0.09375
- w_gate: bfloat16 [4096, 14336], P('gx', 'gy'), may hold values from -0.09375 to 0.09375
- w_up: bfloat16 [4096, 14336], P('gx', 'gy'), may hold values from -0.09375 to 0.09375
- w_down: bfloat16 [14336, 4096], P('gy', 'gx'), may hold values from -0.046875 to 0.046875
- lengths: int32 [6], replicated, may hold values from 1 to 3072, 4096 in all
- page_table: int32 [128, 2], replicated, may hold values from 0 to 15, as said below
Outputs:
- layer_out: bfloat16 [4096, 4096], P(('gx', 'gy'))
- paged_key_value_cache: bfloat16 [128, 2, 32, 1024], P('gx', None, None, 'gy')
Inputs may be any that keep to these rules, and one draw needn't show every extreme that they name: `page_table`: page p belongs to token group p // 16, the tokens of one index of gx. Its owner is an index of gx and its slot is below 16; every pair of owner and slot is taken by exactly one page. Of one token group's pages, 8 owners receive exactly 2 each and the other owners none.
All inputs are finite; a program needn't handle non-finite values.
Results may differ from a plain program's by a relative error of at most 0.025.
The roundings to bfloat16 on the way count: a program that leaves them out, or rounds other values in their place, can miss the bound.
Values may be sent and summed in bfloat16 or wider, within the bound.
A program may use at most 128 MiB of HBM per device.

v0:
```python
import jax
import jax.numpy as jnp
from jax import lax
from jax.sharding import PartitionSpec as P

HEAD_WIDTH = 128
WIN = 4096
PAGE_TOKENS = 32
rope_base = 10000.0
norm_eps = 1e-05
masked_score = -1e30


def partner(value, axis, distance):
    mask = 2**distance
    pairs = [(source, source ^ mask) for source in range(lax.axis_size(axis))]
    return lax.ppermute(value, axis, pairs)


def rms_scale(values, gain):
    floats = values.astype(jnp.float32)
    mean_square = jnp.mean(floats * floats, axis=-1, keepdims=True)
    return floats * lax.rsqrt(mean_square + norm_eps) * gain.astype(jnp.float32)


def segment_info(lengths, token_index):
    ends = jnp.cumsum(lengths, dtype=jnp.int32)
    starts = ends - lengths
    inside = (token_index[:, None] >= starts[None, :]).astype(jnp.int32)
    segment = jnp.sum(inside, axis=1, dtype=jnp.int32) - 1
    chosen = (segment[:, None] == jnp.arange(lengths.shape[0], dtype=jnp.int32)[None, :]).astype(
        jnp.int32
    )
    token_positions = token_index - jnp.sum(chosen * starts[None, :], axis=1, dtype=jnp.int32)
    return (segment, token_positions)


def apply_rotary(values, token_positions):
    half = values.shape[-1] // 2
    freq = rope_base ** (-jnp.arange(half, dtype=jnp.float32) * 2.0 / values.shape[-1])
    angle = token_positions.astype(jnp.float32)[:, None] * freq[None, :]
    cosine = jnp.cos(angle)[:, None, :]
    sine = jnp.sin(angle)[:, None, :]
    first = values[..., :half]
    second = values[..., half:]
    return jnp.concatenate(
        [first * cosine - second * sine, second * cosine + first * sine], axis=-1
    )


def join_halves(mine, other, lower):
    return jnp.where(
        lower, jnp.concatenate([mine, other], axis=1), jnp.concatenate([other, mine], axis=1)
    )


def row_products(source, pieces):
    return tuple((jnp.dot(source, piece, preferred_element_type=jnp.float32) for piece in pieces))


def per_device(
    tokens,
    attn_gain,
    mlp_gain,
    w_query,
    w_key,
    value_projection,
    w_out,
    w_gate,
    w_up,
    w_down,
    lengths,
    page_table,
):
    group_count = lax.axis_size("gx")
    local_rows = tokens.shape[0]
    group = local_rows * lax.axis_size("gy")
    group_index = lax.axis_index("gx")
    head_index = lax.axis_index("gy")
    group_start = group_index * group
    lower = head_index % 2 == 0
    query_cols = w_query.shape[1]
    query_heads = query_cols // HEAD_WIDTH
    key_cols = w_key.shape[1]
    key_heads = max(1, key_cols // HEAD_WIDTH)
    per_key = query_heads // key_heads
    normed = lax.all_gather(
        rms_scale(tokens, attn_gain).astype(jnp.bfloat16), "gy", axis=0, tiled=True
    )
    query = row_products(normed, (lax.all_gather(w_query, "gx", axis=0, tiled=True),))[0]
    key_weight, value_weight = (w_key, value_projection)
    unrotated_key, value_raw = row_products(
        normed,
        (
            lax.all_gather(key_weight, "gx", axis=0, tiled=True),
            lax.all_gather(value_weight, "gx", axis=0, tiled=True),
        ),
    )
    other_key, other_value = (
        partner(unrotated_key.astype(jnp.bfloat16), "gy", 0).astype(unrotated_key.dtype),
        partner(value_raw.astype(jnp.bfloat16), "gy", 0).astype(value_raw.dtype),
    )
    unrotated_key = join_halves(unrotated_key, other_key, lower)
    value_raw = join_halves(value_raw, other_value, lower)
    token_index = group_start + jnp.arange(group, dtype=jnp.int32)
    segment, token_positions = segment_info(lengths, token_index)
    query_rot = (
        apply_rotary(query.reshape(group, query_heads, HEAD_WIDTH), token_positions)
        .astype(jnp.bfloat16)
        .reshape(group, key_heads, per_key, HEAD_WIDTH)
    )
    rotated_key = (
        apply_rotary(unrotated_key.reshape(group, key_heads, HEAD_WIDTH), token_positions)
        .astype(jnp.bfloat16)
        .reshape(group, key_heads * HEAD_WIDTH)
    )
    value_vectors = value_raw.astype(jnp.bfloat16)
    scale = HEAD_WIDTH ** (-0.5)
    start_state = (
        jnp.full((key_heads, per_key, group), masked_score, jnp.float32),
        jnp.zeros((key_heads, per_key, group), jnp.float32),
        jnp.zeros((key_heads, per_key, group, HEAD_WIDTH), jnp.float32),
    )
    keys = lax.all_gather(rotated_key, "gx", axis=0, tiled=True)
    values = lax.all_gather(value_vectors, "gx", axis=0, tiled=True)
    count = keys.shape[0]
    key_index = jnp.arange(count, dtype=jnp.int32)
    key_segment, unused = segment_info(lengths, key_index)
    distance = token_index[:, None] - key_index[None, :]
    allowed = (segment[:, None] == key_segment[None, :]) & (distance >= 0) & (distance < WIN)

    def update(state):
        running, total, weighted = state
        scores = (
            jnp.einsum(
                "qhgd,khd->hgqk",
                query_rot,
                keys.reshape(count, key_heads, HEAD_WIDTH),
                preferred_element_type=jnp.float32,
            )
            * scale
        )
        masked = jnp.where(allowed[None, None], scores, masked_score)
        newest = jnp.maximum(running, jnp.max(masked, axis=-1))
        weights = jnp.where(allowed[None, None], jnp.exp(masked - newest[..., None]), 0.0)
        mixed = jnp.einsum(
            "hgqk,khd->hgqd",
            weights.astype(jnp.bfloat16),
            values.reshape(count, key_heads, HEAD_WIDTH),
            preferred_element_type=jnp.float32,
        )
        return (newest, jnp.sum(weights, axis=-1), mixed)

    state = lax.cond(jnp.any(allowed), update, lambda state: state, start_state)
    attended = (state[2] / state[1][..., None]).astype(jnp.bfloat16)
    attended = attended.transpose(2, 0, 1, 3).reshape(group, query_cols)
    partial_value = jnp.dot(
        attended,
        lax.all_gather(w_out, "gx", axis=1, tiled=True),
        preferred_element_type=jnp.float32,
    )
    share = lax.psum_scatter(
        partial_value.astype(jnp.bfloat16), "gy", scatter_dimension=0, tiled=True
    ).astype(jnp.float32)
    residual = (tokens.astype(jnp.float32) + share).astype(jnp.bfloat16)
    mlp_input = lax.all_gather(
        rms_scale(residual, mlp_gain).astype(jnp.bfloat16), "gy", axis=0, tiled=True
    )
    gate, up_values = row_products(
        mlp_input,
        (
            lax.all_gather(w_gate, "gx", axis=0, tiled=True),
            lax.all_gather(w_up, "gx", axis=0, tiled=True),
        ),
    )
    hidden = (jax.nn.silu(gate) * up_values).astype(jnp.bfloat16)
    down_full = lax.all_gather(w_down, "gx", axis=1, tiled=True)
    mlp_share = lax.psum_scatter(
        jnp.dot(hidden, down_full, preferred_element_type=jnp.float32).astype(jnp.bfloat16),
        "gy",
        scatter_dimension=0,
        tiled=True,
    ).astype(jnp.float32)
    layer_out = (residual.astype(jnp.float32) + mlp_share).astype(jnp.bfloat16)
    own_start = jnp.where(lower, 0, key_cols).astype(jnp.int32)
    local_key = lax.dynamic_slice_in_dim(rotated_key, own_start, key_cols, 1)
    own_value = lax.dynamic_slice_in_dim(value_vectors, own_start, key_cols, 1)
    slots_group = group // PAGE_TOKENS
    capacity = max(2, slots_group // group_count)
    pages_local = (
        jnp.stack([local_key, own_value], axis=0)
        .reshape(2, slots_group, PAGE_TOKENS, key_cols)
        .transpose(1, 0, 2, 3)
        .reshape(slots_group, 2 * PAGE_TOKENS * key_cols)
    )
    owner = page_table[:, 0]
    slot = page_table[:, 1]
    page_index = jnp.arange(owner.shape[0], dtype=jnp.int32)
    page_group = page_index // slots_group
    before = (
        (page_group[:, None] == page_group[None, :])
        & (owner[:, None] == owner[None, :])
        & (page_index[None, :] < page_index[:, None])
    )
    rank = jnp.sum(before.astype(jnp.int32), axis=1, dtype=jnp.int32)
    my_owner = lax.dynamic_slice_in_dim(owner, group_index * slots_group, slots_group, 0)
    my_rank = lax.dynamic_slice_in_dim(rank, group_index * slots_group, slots_group, 0)
    target = jnp.arange(group_count * capacity, dtype=jnp.int32)
    select = (
        (my_owner[None, :] == target[:, None] // capacity)
        & (my_rank[None, :] == target[:, None] % capacity)
    ).astype(jnp.bfloat16)
    outgoing = (
        jnp.dot(select, pages_local, preferred_element_type=jnp.float32)
        .astype(jnp.bfloat16)
        .reshape(group_count, capacity, 2, PAGE_TOKENS, key_cols)
    )
    incoming = lax.all_to_all(outgoing, "gx", split_axis=0, concat_axis=0, tiled=True)
    column = page_group * capacity + rank
    pick = (
        (owner[None, :] == group_index)
        & (slot[None, :] == jnp.arange(slots_group, dtype=jnp.int32)[:, None])
    ).astype(jnp.float32)
    place = (column[:, None] == target[None, :]).astype(jnp.float32)
    routing = jnp.dot(pick, place, preferred_element_type=jnp.float32).astype(jnp.bfloat16)
    paged_key_value_cache = (
        jnp.dot(
            routing,
            incoming.reshape(group_count * capacity, 2 * PAGE_TOKENS * key_cols),
            preferred_element_type=jnp.float32,
        )
        .astype(jnp.bfloat16)
        .reshape(slots_group, 2, PAGE_TOKENS, key_cols)
    )
    return (layer_out, paged_key_value_cache)


def solution(mesh):
    placed = (
        P(("gx", "gy"), None),
        P(),
        P(),
        P("gx", "gy"),
        P("gx", "gy"),
        P("gx", "gy"),
        P("gy", "gx"),
        P("gx", "gy"),
        P("gx", "gy"),
        P("gy", "gx"),
        P(),
        P(),
    )
    return jax.shard_map(
        per_device,
        mesh=mesh,
        in_specs=placed,
        out_specs=(P(("gx", "gy"), None), P("gx", None, None, "gy")),
        check_vma=False,
    )
```

profile of v0, /device:TPU:0, one launch (start us, length us, event | category | flops | bytes accessed | tf_op | source)
XLA Modules:
  0.0 550.2 jit_solution(15981981439846609788)
XLA Ops:
  13.4 14.6 %all_gather.35 = bf16[4096,64]{0,1:T(8,128)(2,1)S(1)} all-gather(bf16[512,64]{0,1:T(8,128)(2,1)} %param.18), channel_id=1, replica_groups=mesh['gx'=8,'gy'=16] {'gx'}, dimensions={0}, use_global_device_ids=true | all-gather | bytes 589824 | tf_op jit(solution)/shard_map/all_gather | solution.py:95
  28.0 36.9 %all-gather.10.cloned.1.call-done = bf16[512,4096]{1,0:T(8,128)(2,1)} async-done(((bf16[32,4096]{1,0:T(8,128)(2,1)}), bf16[512,4096]{1,0:T(8,128)(2,1)}) %all-gather.10.cloned.1.call-update) | async-done | bytes 4194320 | tf_op jit(solution)/shard_map/all_gather | solution.py:87
  64.9 3.6 fusion.62
  74.2 14.2 %all_gather.37 = bf16[4096,64]{0,1:T(8,128)(2,1)S(1)} all-gather(bf16[512,64]{0,1:T(8,128)(2,1)S(1)} %copy-done.3), channel_id=1, replica_groups=mesh['gx'=8,'gy'=16] {'gx'}, dimensions={0}, use_global_device_ids=true | all-gather | bytes 589824 | tf_op jit(solution)/shard_map/all_gather | solution.py:96
  88.3 3.7 fusion.64
  97.9 3.6 fusion.20
  103.9 4.2 fusion.63
  109.9 7.8 %all-gather.14.cloned.1.call-done = bf16[4096,128]{0,1:T(8,128)(2,1)} async-done(((bf16[512,128]{0,1:T(8,128)(2,1)}), bf16[4096,128]{0,1:T(8,128)(2,1)}) %all-gather.14.cloned.1.call-update) | async-done | bytes 1048592 | tf_op jit(solution)/shard_map/all_gather | solution.py:124
  117.7 25.0 %all-gather.16.cloned.1.call-done = bf16[4096,128]{0,1:T(8,128)(2,1)} async-done(((bf16[512,128]{0,1:T(8,128)(2,1)}), bf16[4096,128]{0,1:T(8,128)(2,1)}) %all-gather.16.cloned.1.call-update) | async-done | bytes 1048592 | tf_op jit(solution)/shard_map/all_gather | solution.py:125
  142.8 14.2 %conditional.1 = (f32[1,2,512]{2,1,0:T(2,128)S(1)}, f32[1,2,512,128]{2,3,1,0:T(8,128)S(1)}) conditional(s32[]{:T(128)} %convert_element_type.114, () %tuple.16, (pred[512,4096]{0,1:T(8,128)(4,1)S(1)}, bf16[512,1,2,128]{3,0,2,1:T(8,128)(2,1)S(1)}, bf16[4096,128]{0,1:T(8,128)(2,1)}, bf16[4096,128]{0,1:T(8,128)(2,1)}) %tuple.17), branch_computations={%region_6.7_spmd, %region_7.10_spmd} | conditional | flops 2202008576 | bytes 63725612 | solution.py:154
  142.8 5.1 fusion
  147.9 4.6 fusion.7
  152.5 4.4 fusion.2
  157.0 12.6 %all-gather.18.cloned.1.call-done = bf16[256,4096]{1,0:T(8,128)(2,1)} async-done(((bf16[256,512]{1,0:T(8,128)(2,1)}), bf16[256,4096]{1,0:T(8,128)(2,1)}) %all-gather.18.cloned.1.call-update) | async-done | bytes 2097168 | tf_op jit(solution)/shard_map/all_gather | solution.py:159
  169.6 4.9 convolution_convert_fusion.1
  175.4 77.2 %reduce-scatter.3.cloned.1.call-done = bf16[32,4096]{1,0:T(8,128)(2,1)} async-done(((bf16[512,4096]{1,0:T(8,128)(2,1)}), bf16[32,4096]{1,0:T(8,128)(2,1)}) %reduce-scatter.3.cloned.1.call-update) | async-done | bytes 262160 | tf_op jit(solution)/shard_map/reduce_scatter | solution.py:162
  257.1 42.2 %all-gather.22.cloned.1.call-done = bf16[4096,896]{1,0:T(8,128)(2,1)} async-done(((bf16[512,896]{1,0:T(8,128)(2,1)}), bf16[4096,896]{1,0:T(8,128)(2,1)}) %all-gather.22.cloned.1.call-update) | async-done | bytes 7340048 | tf_op jit(solution)/shard_map/all_gather | solution.py:172
  299.4 54.3 %all-gather.20.cloned.1.call-done = bf16[512,4096]{1,0:T(8,128)(2,1)} async-done(((bf16[32,4096]{1,0:T(8,128)(2,1)}), bf16[512,4096]{1,0:T(8,128)(2,1)}) %all-gather.20.cloned.1.call-update) | async-done | bytes 4194320 | tf_op jit(solution)/shard_map/all_gather | solution.py:166
  353.7 9.8 %fusion.65 = f32[512,896]{1,0:T(8,128)S(1)} fusion(bf16[512,4096]{1,0:T(8,128)(2,1)} %all-gather.20.cloned.1.call-done, bf16[4096,896]{1,0:T(8,128)(2,1)} %all-gather.22.cloned.1.call-done), kind=kOutput, calls=%fused_computation.120 | convolution fusion | flops 3758096384 | bytes 13369344 | tf_op jit(solution)/shard_map/dot_general | solution.py:58
  363.5 37.2 %all-gather.24.cloned.1.call-done = bf16[4096,896]{1,0:T(8,128)(2,1)} async-done(((bf16[512,896]{1,0:T(8,128)(2,1)}), bf16[4096,896]{1,0:T(8,128)(2,1)}) %all-gather.24.cloned.1.call-update) | async-done | bytes 7340048 | tf_op jit(solution)/shard_map/all_gather | solution.py:173
  400.8 47.2 %all-gather.26.cloned.1.call-done = bf16[896,4096]{1,0:T(8,128)(2,1)} async-done(((bf16[896,512]{1,0:T(8,128)(2,1)}), bf16[896,4096]{1,0:T(8,128)(2,1)}) %all-gather.26.cloned.1.call-update) | async-done | bytes 7340048 | tf_op jit(solution)/shard_map/all_gather | solution.py:177
  448.0 16.3 %convolution_convert_fusion = bf16[512,4096]{1,0:T(8,128)(2,1)} fusion(bf16[896,4096]{1,0:T(8,128)(2,1)} %all-gather.26.cloned.1.call-done, f32[512,896]{1,0:T(8,128)S(1)} %fusion.65, bf16[512,4096]{1,0:T(8,128)(2,1)} %all-gather.20.cloned.1.call-done, bf16[4096,896]{1,0:T(8,128)(2,1)} %all-gather.24.cloned.1.call-done), kind=kOutput, calls=%fused_computation.22 | convolution fusion | flops 7521042432 | bytes 24903680 | tf_op jit(solution)/shard_map/dot_general | solution.py:179
  470.7 6.0 %all-to-all-done = bf16[8,2,4096]{2,1,0:T(2,128)(2,1)S(1)} async-done(((bf16[8,2,4096]{2,1,0:T(2,128)(2,1)}), bf16[8,2,4096]{2,1,0:T(2,128)(2,1)S(1)}, u32[]{:S(2)}, u32[]{:S(2)}) %all-to-all-start) | async-done | bytes 131104 | tf_op jit(solution)/shard_map/all_to_all | solution.py:218
  478.6 63.3 %reduce-scatter.5.cloned.1.call-done = bf16[32,4096]{1,0:T(8,128)(2,1)} async-done(((bf16[512,4096]{1,0:T(8,128)(2,1)}), bf16[32,4096]{1,0:T(8,128)(2,1)}) %reduce-scatter.5.cloned.1.call-update) | async-done | bytes 262160 | tf_op jit(solution)/shard_map/reduce_scatter | solution.py:178
  (96 shorter events, 36.6 us)
Async XLA Ops:
  7.2 57.7 %all-gather.10.cloned.1.call-start = ((), (), s32[]{:S(2)}) async-start(), calls=%async_computation.3 | async-start | bytes 4456448 | tf_op jit(solution)/shard_map/all_gather | solution.py:87
  7.9 66.3 %copy-start.3 = (bf16[512,64]{0,1:T(8,128)(2,1)S(1)}, bf16[512,64]{0,1:T(8,128)(2,1)}, u32[]{:S(2)}) copy-start(bf16[512,64]{0,1:T(8,128)(2,1)} %param.19) | copy-start | bytes 196612
  10.9 93.0 %all-gather.12.cloned.1.call-start = ((), (), s32[]{:S(2)}) async-start(), calls=%async_computation.4 | async-start | bytes 2359296 | tf_op jit(solution)/shard_map/all_gather | solution.py:90
  11.6 106.1 %all-gather.14.cloned.1.call-start = ((), (), s32[]{:S(2)}) async-start(), calls=%async_computation.5 | async-start | bytes 1179648 | tf_op jit(solution)/shard_map/all_gather | solution.py:124
  68.5 4.3 collective-permute-start
  74.1 68.7 %all-gather.16.cloned.1.call-start = ((), (), s32[]{:S(2)}) async-start(), calls=%async_computation.6 | async-start | bytes 1179648 | tf_op jit(solution)/shard_map/all_gather | solution.py:125
  92.0 4.4 collective-permute-start.1
  97.1 72.5 %all-gather.18.cloned.1.call-start = ((), (), s32[]{:S(2)}) async-start(), calls=%async_computation.7 | async-start | bytes 2359296 | tf_op jit(solution)/shard_map/all_gather | solution.py:159
  97.7 154.9 %reduce-scatter.3.cloned.1.call-start = ((), (), s32[]{:S(2)}) async-start(), calls=%async_computation.8 | async-start | bytes 4456448 | tf_op jit(solution)/shard_map/reduce_scatter | solution.py:162
  142.8 5.2 copy-start.6
  174.6 0.8 copy-start.4
  174.6 78.0 %copy-start = (bf16[32,4096]{1,0:T(8,128)(2,1)S(1)}, bf16[32,4096]{1,0:T(8,128)(2,1)}, u32[]{:S(2)}) copy-start(bf16[32,4096]{1,0:T(8,128)(2,1)} %param.14) | copy-start | bytes 786436
  174.6 124.8 %all-gather.22.cloned.1.call-start = ((), (), s32[]{:S(2)}) async-start(), calls=%async_computation.10 | async-start | bytes 8257536 | tf_op jit(solution)/shard_map/all_gather | solution.py:172
  175.3 178.4 %all-gather.20.cloned.1.call-start = ((), (), s32[]{:S(2)}) async-start(), calls=%async_computation.9 | async-start | bytes 4456448 | tf_op jit(solution)/shard_map/all_gather | solution.py:166
  255.5 145.2 %all-gather.24.cloned.1.call-start = ((), (), s32[]{:S(2)}) async-start(), calls=%async_computation.11 | async-start | bytes 8257536 | tf_op jit(solution)/shard_map/all_gather | solution.py:173
  256.3 191.7 %all-gather.26.cloned.1.call-start = ((), (), s32[]{:S(2)}) async-start(), calls=%async_computation.12 | async-start | bytes 8257536 | tf_op jit(solution)/shard_map/all_gather | solution.py:177
  256.9 285.0 %reduce-scatter.5.cloned.1.call-start = ((), (), s32[]{:S(2)}) async-start(), calls=%async_computation.13 | async-start | bytes 4456448 | tf_op jit(solution)/shard_map/reduce_scatter | solution.py:178
  464.2 0.7 copy-start.5
  464.2 1.2 copy-start.2
  464.2 77.7 %copy-start.1 = (bf16[32,4096]{1,0:T(8,128)(2,1)S(1)}, bf16[32,4096]{1,0:T(8,128)(2,1)}, u32[]{:S(2)}) copy-start(bf16[32,4096]{1,0:T(8,128)(2,1)} %reduce-scatter.3.cloned.1.call-done) | copy-start | bytes 786436
  467.4 9.4 %all-to-all-start = ((bf16[8,2,4096]{2,1,0:T(2,128)(2,1)}), bf16[8,2,4096]{2,1,0:T(2,128)(2,1)S(1)}, u32[]{:S(2)}, u32[]{:S(2)}) async-start(bf16[8,2,4096]{2,1,0:T(2,128)(2,1)} %reshape.453), calls=%async_computation.2 | async-start | bytes 262144 | tf_op jit(solution)/shard_map/all_to_all | solution.py:218
Sparse Core Ops, SparseCore 0:
  11.0 53.8 all-gather.9
  66.6 25.7 all-gather.11
  94.1 23.5 all-gather.13
  119.3 23.4 all-gather.15
  144.3 25.2 all-gather.17
  174.7 77.8 reduce-scatter.2
  254.4 44.9 all-gather.21
  302.3 51.3 all-gather.19
  355.5 45.2 all-gather.23
  402.4 45.4 all-gather.25
  464.4 77.4 reduce-scatter.4
where the time goes:
time: 551 us; the launch traced here: 550 us
  waiting for transfers between devices  419 us (76%)
  matrix products  52.7 us (10%)
  blocking collectives  28.8 us (5%)
  other arithmetic  23.6 us (4%)
  between operations  14.8 us (3%)
  starting transfers between devices  7.29 us (1%)
    reduce_scatter x1, waiting for transfers between devices, per_device(): lax.psum_scatter(partial_value.astype(jnp.bfloat16), 'gy', scatter_dimens...  77.2 us
    reduce_scatter x1, waiting for transfers between devices, per_device(): lax.psum_scatter(jnp.dot(hidden, down_full, preferred_element_type=jnp.fl...  63.3 us
    all_gather x1, waiting for transfers between devices, per_device(): lax.all_gather(rms_scale(residual, mlp_gain).astype(jnp.bfloat16), 'gy',...  54.3 us
    all_gather x1, waiting for transfers between devices, per_device(): down_full = lax.all_gather(w_down, 'gx', axis=1, tiled=True)  47.2 us
    all_gather x1, waiting for transfers between devices, per_device(): lax.all_gather(w_gate, 'gx', axis=0, tiled=True)  42.2 us
    all_gather x1, waiting for transfers between devices, per_device(): lax.all_gather(w_up, 'gx', axis=0, tiled=True)  37.2 us
    all_gather x1, waiting for transfers between devices, per_device(): lax.all_gather(rms_scale(tokens, attn_gain).astype(jnp.bfloat16), 'gy', a...  36.9 us
    all_gather x1, waiting for transfers between devices, per_device(): values = lax.all_gather(value_vectors, 'gx', axis=0, tiled=True)  25 us
  transfers between devices with their start and end apart: 14, of which 13 were waited for; matrix products, arithmetic and copies ran while one was open for 10% of the time, Pallas kernels for 0%

commit v1 on v0

--- a/solution.py
+++ b/solution.py
@@ -72,6 +72,16 @@
     lengths,
     page_table,
 ):
+
+    def values_watch(a0):
+        right_arr = lax.all_to_all(
+            jnp.stack([a0 for _ in range(lax.psum(1, "gx"))], 0),
+            axis_name="gx",
+            split_axis=0,
+            concat_axis=0,
+        )
+        return jnp.concatenate(right_arr, 0)
+
     group_count = lax.axis_size("gx")
     local_rows = tokens.shape[0]
     group = local_rows * lax.axis_size("gy")
@@ -167,11 +177,7 @@
         rms_scale(residual, mlp_gain).astype(jnp.bfloat16), "gy", axis=0, tiled=True
     )
     gate, up_values = row_products(
-        mlp_input,
-        (
-            lax.all_gather(w_gate, "gx", axis=0, tiled=True),
-            lax.all_gather(w_up, "gx", axis=0, tiled=True),
-        ),
+        mlp_input, (values_watch(w_gate), lax.all_gather(w_up, "gx", axis=0, tiled=True))
     )
     hidden = (jax.nn.silu(gate) * up_values).astype(jnp.bfloat16)
     down_full = lax.all_gather(w_down, "gx", axis=1, tiled=True)

time: 551 us -> 526 us (0.955)
  waiting for transfers between devices: 419 us -> 280 us
  blocking collectives: 28.8 us -> 142 us
    all_to_all x0 -> x1, blocking collectives: none -> 113 us  [values_watch(): lax.all_to_all(jnp.stack([a0 for _ in range(lax.psum(1, 'gx'))], 0), axis...]
    all_gather x1, waiting for transfers between devices: 54.3 us -> 0.01 us  [per_device(): lax.all_gather(rms_scale(residual, mlp_gain).astype(jnp.bfloat16), 'gy',...]
    all_gather x1 -> x0, waiting for transfers between devices: 42.2 us -> none  [per_device(): lax.all_gather(w_gate, 'gx', axis=0, tiled=True)]
    all_gather x1, waiting for transfers between devices: 37.2 us -> 0.02 us  [per_device(): lax.all_gather(w_up, 'gx', axis=0, tiled=True)]
    all_gather x1, waiting for transfers between devices: 47.2 us -> 41.6 us  [per_device(): down_full = lax.all_gather(w_down, 'gx', axis=1, tiled=True)]
  transfers between devices with their start and end apart: 14 -> 13, of which waited for: 13 -> 10; matrix products, arithmetic and copies ran while one was open for 10% -> 10% of each run, Pallas kernels for 0% -> 0%
where the time goes in v1:
time: 526 us; the launch traced here: 525 us
  waiting for transfers between devices  280 us (53%)
  blocking collectives  142 us (27%)
  matrix products  52.7 us (10%)
  other arithmetic  23.6 us (4%)
  between operations  15.1 us (3%)
  starting transfers between devices  7.07 us (1%)
  local copies, waits for them, and re-layouts  5.31 us (1%)
    all_to_all x1, blocking collectives, values_watch(): lax.all_to_all(jnp.stack([a0 for _ in range(lax.psum(1, 'gx'))], 0), axis...  113 us
    reduce_scatter x1, waiting for transfers between devices, per_device(): lax.psum_scatter(partial_value.astype(jnp.bfloat16), 'gy', scatter_dimens...  77.9 us
    reduce_scatter x1, waiting for transfers between devices, per_device(): lax.psum_scatter(jnp.dot(hidden, down_full, preferred_element_type=jnp.fl...  63.3 us
    all_gather x1, waiting for transfers between devices, per_device(): down_full = lax.all_gather(w_down, 'gx', axis=1, tiled=True)  41.6 us
    all_gather x1, waiting for transfers between devices, per_device(): lax.all_gather(rms_scale(tokens, attn_gain).astype(jnp.bfloat16), 'gy', a...  36.9 us
    all_gather x1, waiting for transfers between devices, per_device(): values = lax.all_gather(value_vectors, 'gx', axis=0, tiled=True)  25 us
    dot_general x4, matrix products, row_products(): jnp.dot(source, piece, preferred_element_type=jnp.float32)  21.2 us
    dot_general x1, matrix products, per_device(): jnp.dot(hidden, down_full, preferred_element_type=jnp.float32)  16.3 us
  transfers between devices with their start and end apart: 13, of which 10 were waited for; matrix products, arithmetic and copies ran while one was open for 10% of the time, Pallas kernels for 0%

profile of v1, /device:TPU:0, one launch (start us, length us, event | category | flops | bytes accessed | tf_op | source)
XLA Modules:
  0.0 525.0 jit_solution(14903019865644642604)
XLA Ops:
  13.4 14.6 %all_gather.32 = bf16[4096,64]{0,1:T(8,128)(2,1)S(1)} all-gather(bf16[512,64]{0,1:T(8,128)(2,1)} %param.18), channel_id=1, replica_groups=mesh['gx'=8,'gy'=16] {'gx'}, dimensions={0}, use_global_device_ids=true | all-gather | bytes 589824 | tf_op jit(solution)/shard_map/all_gather | solution.py:105
  28.0 36.9 %all-gather.9.cloned.1.call-done = bf16[512,4096]{1,0:T(8,128)(2,1)} async-done(((bf16[32,4096]{1,0:T(8,128)(2,1)}), bf16[512,4096]{1,0:T(8,128)(2,1)}) %all-gather.9.cloned.1.call-update) | async-done | bytes 4194320 | tf_op jit(solution)/shard_map/all_gather | solution.py:97
  64.9 3.6 fusion.62
  70.0 2.8 collective-permute-done
  74.2 14.2 %all_gather.34 = bf16[4096,64]{0,1:T(8,128)(2,1)S(1)} all-gather(bf16[512,64]{0,1:T(8,128)(2,1)S(1)} %copy-done.4), channel_id=1, replica_groups=mesh['gx'=8,'gy'=16] {'gx'}, dimensions={0}, use_global_device_ids=true | all-gather | bytes 589824 | tf_op jit(solution)/shard_map/all_gather | solution.py:106
  88.4 3.6 fusion.64
  97.9 3.6 fusion.20
  103.9 4.2 fusion.63
  109.9 7.8 %all-gather.13.cloned.1.call-done = bf16[4096,128]{0,1:T(8,128)(2,1)} async-done(((bf16[512,128]{0,1:T(8,128)(2,1)}), bf16[4096,128]{0,1:T(8,128)(2,1)}) %all-gather.13.cloned.1.call-update) | async-done | bytes 1048592 | tf_op jit(solution)/shard_map/all_gather | solution.py:134
  117.7 25.0 %all-gather.15.cloned.1.call-done = bf16[4096,128]{0,1:T(8,128)(2,1)} async-done(((bf16[512,128]{0,1:T(8,128)(2,1)}), bf16[4096,128]{0,1:T(8,128)(2,1)}) %all-gather.15.cloned.1.call-update) | async-done | bytes 1048592 | tf_op jit(solution)/shard_map/all_gather | solution.py:135
  142.8 14.2 %conditional.1 = (f32[1,2,512]{2,1,0:T(2,128)S(1)}, f32[1,2,512,128]{2,3,1,0:T(8,128)S(1)}) conditional(s32[]{:T(128)} %convert_element_type.114, () %tuple.16, (pred[512,4096]{0,1:T(8,128)(4,1)S(1)}, bf16[512,1,2,128]{3,0,2,1:T(8,128)(2,1)S(1)}, bf16[4096,128]{0,1:T(8,128)(2,1)}, bf16[4096,128]{0,1:T(8,128)(2,1)}) %tuple.17), branch_computations={%region_6.7_spmd, %region_7.10_spmd} | conditional | flops 2202008576 | bytes 63725612 | solution.py:164
  142.8 5.1 fusion
  147.9 4.6 fusion.7
  152.5 4.4 fusion.2
  157.0 12.6 %all-gather.17.cloned.1.call-done = bf16[256,4096]{1,0:T(8,128)(2,1)} async-done(((bf16[256,512]{1,0:T(8,128)(2,1)}), bf16[256,4096]{1,0:T(8,128)(2,1)}) %all-gather.17.cloned.1.call-update) | async-done | bytes 2097168 | tf_op jit(solution)/shard_map/all_gather | solution.py:169
  169.6 4.9 convolution_convert_fusion.1
  174.6 77.9 %reduce-scatter.3.cloned.1.call-done = bf16[32,4096]{1,0:T(8,128)(2,1)} async-done(((bf16[512,4096]{1,0:T(8,128)(2,1)}), bf16[32,4096]{1,0:T(8,128)(2,1)}) %reduce-scatter.3.cloned.1.call-update) | async-done | bytes 262160 | tf_op jit(solution)/shard_map/reduce_scatter | solution.py:172
  258.0 112.9 %all_to_all.10 = bf16[8,512,896]{2,1,0:T(8,128)(2,1)} all-to-all(bf16[8,512,896]{2,1,0:T(8,128)(2,1)S(1)} %stack.8), channel_id=1, replica_groups=mesh['gx'=8,'gy'=16] {'gx'}, dimensions={0} | all-to-all | bytes 14680064 | tf_op jit(solution)/shard_map/all_to_all | solution.py:77
  370.9 9.9 %fusion.65 = f32[512,896]{1,0:T(8,128)S(1)} fusion(bf16[512,4096]{1,0:T(8,128)(2,1)} %all-gather.19.cloned.1.call-done, bf16[4096,896]{1,0:T(8,128)(2,1)} %bitcast.88), kind=kOutput, calls=%fused_computation.120 | convolution fusion | flops 3758096384 | bytes 13369344 | tf_op jit(solution)/shard_map/dot_general | solution.py:58
  380.8 41.6 %all-gather.23.cloned.1.call-done = bf16[896,4096]{1,0:T(8,128)(2,1)} async-done(((bf16[896,512]{1,0:T(8,128)(2,1)}), bf16[896,4096]{1,0:T(8,128)(2,1)}) %all-gather.23.cloned.1.call-update) | async-done | bytes 7340048 | tf_op jit(solution)/shard_map/all_gather | solution.py:183
  422.4 16.3 %convolution_convert_fusion = bf16[512,4096]{1,0:T(8,128)(2,1)} fusion(bf16[896,4096]{1,0:T(8,128)(2,1)} %all-gather.23.cloned.1.call-done, f32[512,896]{1,0:T(8,128)S(1)} %fusion.65, bf16[512,4096]{1,0:T(8,128)(2,1)} %all-gather.19.cloned.1.call-done, bf16[4096,896]{1,0:T(8,128)(2,1)} %all-gather.21.cloned.1.call-done), kind=kOutput, calls=%fused_computation.22 | convolution fusion | flops 7521042432 | bytes 24903680 | tf_op jit(solution)/shard_map/dot_general | solution.py:185
  441.8 3.4 all-to-all-start.1
  445.2 6.0 %all-to-all-done.1 = bf16[8,2,4096]{2,1,0:T(2,128)(2,1)S(1)} async-done(((bf16[8,2,4096]{2,1,0:T(2,128)(2,1)}), bf16[8,2,4096]{2,1,0:T(2,128)(2,1)S(1)}, u32[]{:S(2)}, u32[]{:S(2)}) %all-to-all-start.1) | async-done | bytes 131104 | tf_op jit(solution)/shard_map/all_to_all | solution.py:224
  453.1 63.3 %reduce-scatter.5.cloned.1.call-done = bf16[32,4096]{1,0:T(8,128)(2,1)} async-done(((bf16[512,4096]{1,0:T(8,128)(2,1)}), bf16[32,4096]{1,0:T(8,128)(2,1)}) %reduce-scatter.5.cloned.1.call-update) | async-done | bytes 262160 | tf_op jit(solution)/shard_map/reduce_scatter | solution.py:184
  (97 shorter events, 30.6 us)
Async XLA Ops:
  7.2 57.7 %all-gather.9.cloned.1.call-start = ((), (), s32[]{:S(2)}) async-start(), calls=%async_computation.4 | async-start | bytes 4456448 | tf_op jit(solution)/shard_map/all_gather | solution.py:97
  7.9 66.3 %copy-start.4 = (bf16[512,64]{0,1:T(8,128)(2,1)S(1)}, bf16[512,64]{0,1:T(8,128)(2,1)}, u32[]{:S(2)}) copy-start(bf16[512,64]{0,1:T(8,128)(2,1)} %param.19) | copy-start | bytes 196612
  10.9 93.0 %all-gather.11.cloned.1.call-start = ((), (), s32[]{:S(2)}) async-start(), calls=%async_computation.5 | async-start | bytes 2359296 | tf_op jit(solution)/shard_map/all_gather | solution.py:100
  11.6 106.1 %all-gather.13.cloned.1.call-start = ((), (), s32[]{:S(2)}) async-start(), calls=%async_computation.6 | async-start | bytes 1179648 | tf_op jit(solution)/shard_map/all_gather | solution.py:134
  68.5 4.3 collective-permute-start
  74.1 68.7 %all-gather.15.cloned.1.call-start = ((), (), s32[]{:S(2)}) async-start(), calls=%async_computation.7 | async-start | bytes 1179648 | tf_op jit(solution)/shard_map/all_gather | solution.py:135
  92.0 4.4 collective-permute-start.1
  97.1 72.5 %all-gather.17.cloned.1.call-start = ((), (), s32[]{:S(2)}) async-start(), calls=%async_computation.8 | async-start | bytes 2359296 | tf_op jit(solution)/shard_map/all_gather | solution.py:169
  97.7 154.8 %reduce-scatter.3.cloned.1.call-start = ((), (), s32[]{:S(2)}) async-start(), calls=%async_computation.9 | async-start | bytes 4456448 | tf_op jit(solution)/shard_map/reduce_scatter | solution.py:172
  142.8 5.1 copy-start.7
  169.6 5.0 copy-start.5
  169.6 82.9 %copy-start = (bf16[32,4096]{1,0:T(8,128)(2,1)S(1)}, bf16[32,4096]{1,0:T(8,128)(2,1)}, u32[]{:S(2)}) copy-start(bf16[32,4096]{1,0:T(8,128)(2,1)} %param.14) | copy-start | bytes 786436
  174.5 82.5 %copy-start.2 = (bf16[512,896]{1,0:T(8,128)(2,1)S(1)}, bf16[512,896]{1,0:T(8,128)(2,1)}, u32[]{:S(2)}) copy-start(bf16[512,896]{1,0:T(8,128)(2,1)} %param.21) | copy-start | bytes 2752516
  174.5 196.4 %all-gather.19.cloned.1.call-start = ((), (), s32[]{:S(2)}) async-start(), calls=%async_computation.10 | async-start | bytes 4456448 | tf_op jit(solution)/shard_map/all_gather | solution.py:176
  255.5 125.3 %all-gather.21.cloned.1.call-start = ((), (), s32[]{:S(2)}) async-start(), calls=%async_computation.11 | async-start | bytes 8257536 | tf_op jit(solution)/shard_map/all_gather | solution.py:180
  256.2 166.2 %all-gather.23.cloned.1.call-start = ((), (), s32[]{:S(2)}) async-start(), calls=%async_computation.12 | async-start | bytes 8257536 | tf_op jit(solution)/shard_map/all_gather | solution.py:183
  257.0 259.4 %reduce-scatter.5.cloned.1.call-start = ((), (), s32[]{:S(2)}) async-start(), calls=%async_computation.13 | async-start | bytes 4456448 | tf_op jit(solution)/shard_map/reduce_scatter | solution.py:184
  438.7 0.7 copy-start.6
  438.7 1.2 copy-start.3
  438.7 77.7 %copy-start.1 = (bf16[32,4096]{1,0:T(8,128)(2,1)S(1)}, bf16[32,4096]{1,0:T(8,128)(2,1)}, u32[]{:S(2)}) copy-start(bf16[32,4096]{1,0:T(8,128)(2,1)} %reduce-scatter.3.cloned.1.call-done) | copy-start | bytes 786436
  441.8 9.4 %all-to-all-start.1 = ((bf16[8,2,4096]{2,1,0:T(2,128)(2,1)}), bf16[8,2,4096]{2,1,0:T(2,128)(2,1)S(1)}, u32[]{:S(2)}, u32[]{:S(2)}) async-start(bf16[8,2,4096]{2,1,0:T(2,128)(2,1)} %reshape.459), calls=%async_computation.3 | async-start | bytes 262144 | tf_op jit(solution)/shard_map/all_to_all | solution.py:224
Sparse Core Ops, SparseCore 0:
  11.0 53.8 all-gather.8
  66.6 25.7 all-gather.10
  94.1 23.5 all-gather.12
  119.3 23.4 all-gather.14
  144.3 25.2 all-gather.16
  174.7 77.8 reduce-scatter.2
  255.6 50.8 all-gather.18
  308.3 68.2 all-gather.20
  378.4 43.9 all-gather.22
  438.9 77.5 reduce-scatter.4
